TPU v7x, 128 devices: a whole 4x4x4 slice. The times are simulated.
128 devices in a mesh: src: 8 (over z, y_hi), rcv: 16 (over x, y_lo, core).
Axes of the slice: x: 4, y: 4 (y_hi: 2, y_lo: 2; y = y_hi * 2 + y_lo), z: 4, core: 2. Of those that a mesh axis runs over, the one named last changes fastest.
Arguments:
- records: bfloat16 [512, 512, 512], P('src', 'rcv'), may hold values from -6 to 6
- surface_operator: float32 [256, 2], replicated, may hold values from -0.7 to 0.7
Outputs:
- multiples: bfloat16 [512, 512, 512], P('src', 'rcv')
All inputs are finite; a program needn't handle non-finite values.
Results may differ from a plain program's by a relative error of at most 0.011.
Values may be sent and summed in bfloat16 or wider, within the bound.
A program may use at most 64 MiB of HBM per device.

v0:
```python
import math

import jax
import jax.numpy as jnp
import numpy as np
from jax import lax
from jax.experimental import pallas as pl
from jax.experimental.pallas import tpu as pltpu
from jax.sharding import PartitionSpec as P

MESH = pl.DeviceIdType.MESH
BF = jnp.bfloat16
F32 = jnp.float32
NS = 512
NT = 512
NF = 256
DEV = 128
A = 8
B = 16


def tables():
    f = np.arange(NF)[:, None]
    t = np.arange(NT)[None, :]
    angle = ((f * t) % NT).astype(np.float32) * np.float32(2.0 * math.pi / NT)
    norm = np.float32(1.0 / math.sqrt(NT))
    cosine, sine = np.cos(angle) * norm, np.sin(angle) * norm
    weight = np.where(f == 0, 1.0, 2.0).astype(np.float32)
    forward = np.stack([cosine, -sine], axis=1).reshape(DEV, 2, 2, NT)
    inverse = np.stack([weight * cosine, -weight * sine], axis=1).reshape(DEV, 2, 2, NT)
    forward = forward.transpose(1, 2, 0, 3).reshape(2 * NF, NT)
    inverse = inverse.transpose(1, 0, 2, 3).reshape(2 * NF, NT)
    return forward, inverse


def swap_matrix():
    m = np.zeros((4, 4, 32, 4, 4, 32), np.float32)
    for x in range(4):
        for y in range(4):
            for r in range(32):
                m[x, y, r, y, x, r] = 1.0
    return m.reshape(512, 512)


def far_first():
    rnd = np.random.RandomState(7)
    all_offsets = [(x, y, z, c) for x in range(4) for y in range(4) for z in range(4) for c in range(2)][1:]
    order = rnd.permutation(len(all_offsets))
    shuffled = [all_offsets[i] for i in order]
    return sorted(shuffled, key=lambda o: -sum(min(v, 4 - v) for v in o[:3]))


def nt(left, right):
    return lax.dot_general(left, right, (((1,), (1,)), ((), ())), preferred_element_type=F32)


def nn(left, right):
    return jnp.dot(left, right, preferred_element_type=F32)


def kernel(
    rec, fwd, inv, eye, swap, coef, out,
    wide, slab, rbuf, spec, q_a, b_one, b_two, pred, rslab, rret, gath, turned,
    fs, fr, bs, br, own,
):
    src, rcv = lax.axis_index("src"), lax.axis_index("rcv")
    me = src * B + rcv
    z, y_hi = src // 2, src % 2
    x, y_lo, core = rcv // 4, (rcv // 2) % 2, rcv % 2
    y = y_hi * 2 + y_lo

    barrier = pltpu.get_barrier_semaphore()

    def greet(i, carry):
        to = me ^ i
        pl.semaphore_signal(barrier, inc=1, device_id=(to // B, to % B), device_id_type=MESH)
        return carry

    lax.fori_loop(1, DEV, greet, 0)

    def dft(pair, carry):
        j = 2 * pair
        traces = jnp.concatenate([rec[16 * q + j + jj] for jj in range(2) for q in range(4)], axis=0)
        for h in range(2):
            o = nt(fwd[256 * h : 256 * (h + 1)], traces)
            for c in range(2):
                for jj in range(2):
                    wide[2 * h + c, pl.ds(j + jj, DEV, stride=16), :] = o[
                        128 * c : 128 * (c + 1), 128 * jj : 128 * (jj + 1)
                    ]
        return carry

    lax.fori_loop(0, 8, dft, 0)

    def pack(i, carry):
        for h in range(2):
            for c in range(2):
                v = wide[2 * h + c, pl.ds(i * 256, 256), :]
                slab[h, pl.ds(i * 16, 16), c] = v.astype(BF).reshape(16, 16, 128)
        return carry

    lax.fori_loop(0, 8, pack, 0)

    pl.semaphore_wait(barrier, DEV - 1)

    xs = [lax.rem(x + d, 4) * 4 for d in range(4)]
    ys = [lax.rem(y + d, 4) for d in range(4)]
    y_s = [v // 2 for v in ys]
    y_r = [(v % 2) * 2 for v in ys]
    zs = [lax.rem(z + d, 4) * 2 for d in range(4)]
    cs = [lax.rem(core + d, 2) for d in range(2)]
    peers = [(zs[o[2]] + y_s[o[1]], xs[o[0]] + y_r[o[1]] + cs[o[3]]) for o in far_first()]

    def forward_sends(h, carry):
        mine = pltpu.make_async_copy(slab.at[h, me], rbuf.at[h, src, rcv], fr.at[h])
        mine.start()
        for a, b in peers:
            pltpu.make_async_remote_copy(
                src_ref=slab.at[h, a * B + b],
                dst_ref=rbuf.at[h, src, rcv],
                send_sem=fs.at[h],
                recv_sem=fr.at[h],
                device_id=(a, b),
                device_id_type=MESH,
            ).start()
        return carry

    lax.fori_loop(0, 2, forward_sends, 0)

    norm = 1.0 / math.sqrt(NS)

    def middle(h, carry):
        pltpu.make_async_copy(rbuf.at[h], rbuf.at[h], fr.at[h]).wait()
        for c in range(2):
            for bb in range(4):
                piece = jnp.concatenate(
                    [rbuf[h, :, 4 * bb + k, c].reshape(128, 128) for k in range(4)], axis=1
                )
                s = nn(piece, swap[...]).astype(BF)
                for q in range(4):
                    spec[c, :, q, :, 128 * bb : 128 * (bb + 1)] = s[:, 128 * q : 128 * (q + 1)].reshape(A, 16, 128)
        for c in range(2):
            for m in range(2):
                for n in range(2):
                    turned_s = nt(eye[...], spec[c, 4 * n : 4 * n + 4, :, :, 256 * m : 256 * (m + 1)].reshape(256, 256))
                    plain = spec[c, 4 * m : 4 * m + 4, :, :, 256 * n : 256 * (n + 1)].reshape(256, 256)
                    q = (0.5 * (plain.astype(F32) + turned_s)).astype(BF)
                    rows, cols = slice(256 * m, 256 * (m + 1)), slice(256 * n, 256 * (n + 1))
                    low, right = slice(512 + 256 * m, 768 + 256 * m), slice(512 + 256 * n, 768 + 256 * n)
                    if c == 0:
                        q_a[rows, cols] = q
                        b_one[rows, cols] = q
                        b_one[low, right] = q
                    else:
                        q_a[rows, right] = q
                        b_one[rows, right] = q
                        b_one[low, cols] = -q
        at = 2 * (2 * me + h)
        k_r, k_i = coef[at] * norm, coef[at + 1] * norm

        def scaled(o):
            r, i = o[:, :512], o[:, 512:]
            return k_r * r - k_i * i, k_r * i + k_i * r

        def product(source, target):
            def rows_of(m, carry2):
                at_m = pl.multiple_of(m * 256, 256)
                r, i = scaled(nn(q_a[pl.ds(at_m, 256), :], source[...]))
                r, i = r.astype(BF), i.astype(BF)
                target[pl.ds(at_m, 256), 0:512] = r
                target[pl.ds(at_m, 256), 512:1024] = i
                target[pl.ds(at_m + 512, 256), 0:512] = -i
                target[pl.ds(at_m + 512, 256), 512:1024] = r
                return carry2

            lax.fori_loop(0, 2, rows_of, 0)

        product(b_one, b_two)
        product(b_two, b_one)

        def last(m, carry2):
            at_m = pl.multiple_of(m * 256, 256)
            third = scaled(nn(q_a[pl.ds(at_m, 256), :], b_one[...]))
            for c in range(2):
                cols = slice(512 * c, 512 * (c + 1))
                total = b_two[pl.ds(at_m, 256), cols].astype(F32) + b_one[pl.ds(at_m, 256), cols].astype(F32) + third[c]
                pred[c, pl.ds(m * 4, 4)] = total.astype(BF).reshape(4, 4, 16, 512)
            return carry2

        lax.fori_loop(0, 2, last, 0)

        for c in range(2):
            for bb in range(4):
                piece = jnp.concatenate(
                    [pred[c, :, q, :, 128 * bb : 128 * (bb + 1)].reshape(128, 128) for q in range(4)], axis=1
                )
                s = nn(piece, swap[...]).astype(BF)
                for k in range(4):
                    rslab[h, :, 4 * bb + k, c] = s[:, 128 * k : 128 * (k + 1)].reshape(A, 16, 128)
        mine = pltpu.make_async_copy(rslab.at[h, src, rcv], rret.at[h, me], br.at[h])
        mine.start()
        for a, b in peers:
            pltpu.make_async_remote_copy(
                src_ref=rslab.at[h, a, b],
                dst_ref=rret.at[h, me],
                send_sem=bs.at[h],
                recv_sem=br.at[h],
                device_id=(a, b),
                device_id_type=MESH,
            ).start()
        return carry

    lax.fori_loop(0, 2, middle, 0)

    def gather(h, carry):
        pltpu.make_async_copy(rret.at[h], rret.at[h], br.at[h]).wait()

        def widen(i, carry2):
            gath[pl.ds(pl.multiple_of(i * 512, 512), 512), :] = rret[h, pl.ds(i * 16, 16)].reshape(512, 128).astype(F32)
            return carry2

        lax.fori_loop(0, 8, widen, 0)

        def turn(j, carry2):
            w = gath[pl.ds(j, 256, stride=16), :].astype(BF)
            turned[h, pl.ds(pl.multiple_of(j * 128, 128), 128), :] = nt(eye[0:128, 0:128], w).astype(BF)
            return carry2

        lax.fori_loop(0, 16, turn, 0)
        return carry

    lax.fori_loop(0, 2, gather, 0)

    def inverse(pair, carry):
        at = pl.multiple_of(pair * 256, 256)
        o = nn(turned[0, pl.ds(at, 256), :], inv[0:256, :]) + nn(turned[1, pl.ds(at, 256), :], inv[256:512, :])
        o = o.astype(BF)
        for jj in range(2):
            for q in range(4):
                out[16 * q + 2 * pair + jj] = o[128 * jj + 32 * q : 128 * jj + 32 * (q + 1), :]
        return carry

    lax.fori_loop(0, 8, inverse, 0)

    whole = pl.ds(0, DEV - 1)
    for h in range(2):
        pltpu.make_async_copy(slab.at[h, whole], slab.at[h, whole], fs.at[h]).wait()
        pltpu.make_async_copy(rret.at[h, whole], rret.at[h, whole], bs.at[h]).wait()


def local(records, surface_operator):
    forward, inverse = tables()
    consts = [jnp.asarray(v).astype(BF) for v in (forward, inverse, np.eye(256, dtype=np.float32), swap_matrix())]
    vmem = pl.BlockSpec(memory_space=pltpu.VMEM)
    return pl.pallas_call(
        kernel,
        name="multiples",
        out_shape=jax.ShapeDtypeStruct((64, 32, NT), BF),
        in_specs=[vmem] * 5 + [pl.BlockSpec(memory_space=pltpu.SMEM)],
        out_specs=vmem,
        scratch_shapes=[
            pltpu.VMEM((4, 2048, 128), F32),
            pltpu.VMEM((2, DEV, 2, 16, 128), BF),
            pltpu.VMEM((2, A, B, 2, 16, 128), BF),
            pltpu.VMEM((2, A, 4, 16, 512), BF),
            pltpu.VMEM((512, 1024), BF),
            pltpu.VMEM((1024, 1024), BF),
            pltpu.VMEM((1024, 1024), BF),
            pltpu.VMEM((2, A, 4, 16, 512), BF),
            pltpu.VMEM((2, A, B, 2, 16, 128), BF),
            pltpu.VMEM((2, DEV, 2, 16, 128), BF),
            pltpu.VMEM((4096, 128), F32),
            pltpu.VMEM((2, 2048, 256), BF),
            pltpu.SemaphoreType.DMA((2,)),
            pltpu.SemaphoreType.DMA((2,)),
            pltpu.SemaphoreType.DMA((2,)),
            pltpu.SemaphoreType.DMA((2,)),
            pltpu.SemaphoreType.DMA((2,)),
        ],
        compiler_params=pltpu.CompilerParams(
            collective_id=0, has_side_effects=True, vmem_limit_bytes=56 * 1024 * 1024
        ),
    )(records, *consts, surface_operator.reshape(2 * NF))


def solution(mesh):
    placed = (P("src", "rcv", None), P())
    return jax.shard_map(
        local, mesh=mesh, in_specs=placed, out_specs=P("src", "rcv", None), check_vma=False
    )
```

profile of v0, /device:TPU:1, one launch (start us, length us, event | category | flops | bytes accessed | tf_op | source)
XLA Modules:
  0.0 77.8 jit_solution(8478796013446110776)
XLA Ops:
  0.0 0.8 %copy.7 = f32[256,2]{1,0:T(8,128)S(1)} copy(f32[256,2]{0,1:T(2,128)} %param.7) | data formatting | bytes 4096 | tf_op args[1]
  0.8 0.7 reshape.3.coef
  1.5 73.1 %multiples.1 = bf16[64,32,512]{2,1,0:T(8,128)(2,1)} custom-call(bf16[64,32,512]{2,1,0:T(8,128)(2,1)} %rec.1, bf16[512,512]{1,0:T(8,128)(2,1)} %constant.12.fwd, bf16[512,512]{1,0:T(8,128)(2,1)} %constant.13.inv, bf16[256,256]{1,0:T(8,128)(2,1)} %constant.14.eye, bf16[512,512]{1,0:T(8,128)(2,1)} %constant.15.swap, f32[512]{0:T(512)} %reshape.3.coef), custom_call_target="tpu_custom_call" | custom-call | tf_op jit(solution)/shard_map/multiples/pallas_call | solution.py:255
  74.7 3.2 %copy.9 = bf16[64,32,512]{2,1,0:T(8,128)(2,1)} copy(bf16[64,32,512]{2,1,0:T(8,128)(2,1)} %multiples.1) | data formatting | bytes 4194304
where the time goes:
time: 78 us; the launch traced here: 77.8 us
  Pallas kernels  73.1 us (94%)
  local copies, waits for them, and re-layouts  4.69 us (6%)
    pallas_call x1, Pallas kernels, local(): pl.pallas_call(kernel, name='multiples', out_shape=jax.ShapeDtypeStruct((...  73.1 us
    unnamed x2, local copies, waits for them, and re-layouts  3.97 us

commit v1 on v0

--- a/solution.py
+++ b/solution.py
@@ -59,10 +59,22 @@
 
 
 def kernel(
-    rec, fwd, inv, eye, swap, coef, out,
+    rec_in, tab_in, coef, out,
+    rec, fwd, inv, eye, swap,
     wide, slab, rbuf, spec, q_a, b_one, b_two, pred, rslab, rret, gath, turned,
-    fs, fr, bs, br, own,
+    fs, fr, bs, br, loaded,
 ):
+    def tab(i):
+        return tab_in.at[pl.ds(512 * i, 512)]
+
+    loads = [
+        pltpu.make_async_copy(here, there, loaded.at[i])
+        for i, (here, there) in enumerate(
+            [(tab(0), fwd), (rec_in, rec), (tab(2), swap), (tab_in.at[pl.ds(1536, 256), pl.ds(0, 256)], eye), (tab(1), inv)]
+        )
+    ]
+    for load in loads:
+        load.start()
     src, rcv = lax.axis_index("src"), lax.axis_index("rcv")
     me = src * B + rcv
     z, y_hi = src // 2, src % 2
@@ -70,38 +82,6 @@
     y = y_hi * 2 + y_lo
 
     barrier = pltpu.get_barrier_semaphore()
-
-    def greet(i, carry):
-        to = me ^ i
-        pl.semaphore_signal(barrier, inc=1, device_id=(to // B, to % B), device_id_type=MESH)
-        return carry
-
-    lax.fori_loop(1, DEV, greet, 0)
-
-    def dft(pair, carry):
-        j = 2 * pair
-        traces = jnp.concatenate([rec[16 * q + j + jj] for jj in range(2) for q in range(4)], axis=0)
-        for h in range(2):
-            o = nt(fwd[256 * h : 256 * (h + 1)], traces)
-            for c in range(2):
-                for jj in range(2):
-                    wide[2 * h + c, pl.ds(j + jj, DEV, stride=16), :] = o[
-                        128 * c : 128 * (c + 1), 128 * jj : 128 * (jj + 1)
-                    ]
-        return carry
-
-    lax.fori_loop(0, 8, dft, 0)
-
-    def pack(i, carry):
-        for h in range(2):
-            for c in range(2):
-                v = wide[2 * h + c, pl.ds(i * 256, 256), :]
-                slab[h, pl.ds(i * 16, 16), c] = v.astype(BF).reshape(16, 16, 128)
-        return carry
-
-    lax.fori_loop(0, 8, pack, 0)
-
-    pl.semaphore_wait(barrier, DEV - 1)
 
     xs = [lax.rem(x + d, 4) * 4 for d in range(4)]
     ys = [lax.rem(y + d, 4) for d in range(4)]
@@ -110,8 +90,34 @@
     zs = [lax.rem(z + d, 4) * 2 for d in range(4)]
     cs = [lax.rem(core + d, 2) for d in range(2)]
     peers = [(zs[o[2]] + y_s[o[1]], xs[o[0]] + y_r[o[1]] + cs[o[3]]) for o in far_first()]
-
-    def forward_sends(h, carry):
+    for to in peers:
+        pl.semaphore_signal(barrier, inc=1, device_id=to, device_id_type=MESH)
+    loads[0].wait()
+    loads[1].wait()
+
+    def dft(h):
+        def step(pair, carry):
+            j = 2 * pair
+            traces = jnp.concatenate([rec[16 * q + j + jj] for jj in range(2) for q in range(4)], axis=0)
+            o = nt(fwd[256 * h : 256 * (h + 1)], traces)
+            for c in range(2):
+                for jj in range(2):
+                    wide[c, pl.ds(j + jj, DEV, stride=16), :] = o[
+                        128 * c : 128 * (c + 1), 128 * jj : 128 * (jj + 1)
+                    ]
+            return carry
+
+        lax.fori_loop(0, 8, step, 0, unroll=4)
+
+        def pack(i, carry):
+            for c in range(2):
+                v = wide[c, pl.ds(i * 256, 256), :]
+                slab[h, pl.ds(i * 16, 16), c] = v.astype(BF).reshape(16, 16, 128)
+            return carry
+
+        lax.fori_loop(0, 8, pack, 0, unroll=2)
+
+    def forward_sends(h):
         mine = pltpu.make_async_copy(slab.at[h, me], rbuf.at[h, src, rcv], fr.at[h])
         mine.start()
         for a, b in peers:
@@ -123,9 +129,14 @@
                 device_id=(a, b),
                 device_id_type=MESH,
             ).start()
-        return carry
-
-    lax.fori_loop(0, 2, forward_sends, 0)
+
+    dft(0)
+    pl.semaphore_wait(barrier, DEV - 1)
+    forward_sends(0)
+    dft(1)
+    forward_sends(1)
+    loads[2].wait()
+    loads[3].wait()
 
     norm = 1.0 / math.sqrt(NS)
 
@@ -155,8 +166,8 @@
                         q_a[rows, right] = q
                         b_one[rows, right] = q
                         b_one[low, cols] = -q
-        at = 2 * (2 * me + h)
-        k_r, k_i = coef[at] * norm, coef[at + 1] * norm
+        at = 2 * me + h
+        k_r, k_i = coef[0, at] * norm, coef[1, at] * norm
 
         def scaled(o):
             r, i = o[:, :512], o[:, 512:]
@@ -219,17 +230,19 @@
             gath[pl.ds(pl.multiple_of(i * 512, 512), 512), :] = rret[h, pl.ds(i * 16, 16)].reshape(512, 128).astype(F32)
             return carry2
 
-        lax.fori_loop(0, 8, widen, 0)
+        lax.fori_loop(0, 8, widen, 0, unroll=2)
 
         def turn(j, carry2):
             w = gath[pl.ds(j, 256, stride=16), :].astype(BF)
             turned[h, pl.ds(pl.multiple_of(j * 128, 128), 128), :] = nt(eye[0:128, 0:128], w).astype(BF)
             return carry2
 
-        lax.fori_loop(0, 16, turn, 0)
+        lax.fori_loop(0, 16, turn, 0, unroll=8)
         return carry
 
     lax.fori_loop(0, 2, gather, 0)
+
+    loads[4].wait()
 
     def inverse(pair, carry):
         at = pl.multiple_of(pair * 256, 256)
@@ -240,7 +253,7 @@
                 out[16 * q + 2 * pair + jj] = o[128 * jj + 32 * q : 128 * jj + 32 * (q + 1), :]
         return carry
 
-    lax.fori_loop(0, 8, inverse, 0)
+    lax.fori_loop(0, 8, inverse, 0, unroll=4)
 
     whole = pl.ds(0, DEV - 1)
     for h in range(2):
@@ -250,16 +263,21 @@
 
 def local(records, surface_operator):
     forward, inverse = tables()
-    consts = [jnp.asarray(v).astype(BF) for v in (forward, inverse, np.eye(256, dtype=np.float32), swap_matrix())]
+    packed = np.concatenate([forward, inverse, swap_matrix(), np.eye(768, 512, dtype=np.float32)])
     vmem = pl.BlockSpec(memory_space=pltpu.VMEM)
     return pl.pallas_call(
         kernel,
         name="multiples",
         out_shape=jax.ShapeDtypeStruct((64, 32, NT), BF),
-        in_specs=[vmem] * 5 + [pl.BlockSpec(memory_space=pltpu.SMEM)],
+        in_specs=[pl.BlockSpec(memory_space=pl.ANY)] * 2 + [pl.BlockSpec(memory_space=pltpu.SMEM)],
         out_specs=vmem,
         scratch_shapes=[
-            pltpu.VMEM((4, 2048, 128), F32),
+            pltpu.VMEM((64, 32, NT), BF),
+            pltpu.VMEM((2 * NF, NT), BF),
+            pltpu.VMEM((2 * NF, NT), BF),
+            pltpu.VMEM((256, 256), BF),
+            pltpu.VMEM((512, 512), BF),
+            pltpu.VMEM((2, 2048, 128), F32),
             pltpu.VMEM((2, DEV, 2, 16, 128), BF),
             pltpu.VMEM((2, A, B, 2, 16, 128), BF),
             pltpu.VMEM((2, A, 4, 16, 512), BF),
@@ -275,12 +293,12 @@
             pltpu.SemaphoreType.DMA((2,)),
             pltpu.SemaphoreType.DMA((2,)),
             pltpu.SemaphoreType.DMA((2,)),
-            pltpu.SemaphoreType.DMA((2,)),
+            pltpu.SemaphoreType.DMA((5,)),
         ],
         compiler_params=pltpu.CompilerParams(
-            collective_id=0, has_side_effects=True, vmem_limit_bytes=56 * 1024 * 1024
+            collective_id=0, has_side_effects=True, vmem_limit_bytes=50 * 1024 * 1024 + 512 * 1024
         ),
-    )(records, *consts, surface_operator.reshape(2 * NF))
+    )(records, jnp.asarray(packed).astype(BF), surface_operator.T)
 
 
 def solution(mesh):

time: 78 us -> 69.7 us (0.89)
  Pallas kernels: 73.1 us -> 67.6 us
  local copies, waits for them, and re-layouts: 4.69 us -> 2 us
    pallas_call x1, Pallas kernels: 73.1 us -> 67.6 us  [local(): pl.pallas_call(kernel, name='multiples', out_shape=jax.ShapeDtypeStruct((...]
    unnamed x2 -> x3, local copies, waits for them, and re-layouts: 3.97 us -> 2 us
where the time goes in v1:
time: 69.7 us; the launch traced here: 69.6 us
  Pallas kernels  67.6 us (97%)
  local copies, waits for them, and re-layouts  2 us (3%)
    pallas_call x1, Pallas kernels, local(): pl.pallas_call(kernel, name='multiples', out_shape=jax.ShapeDtypeStruct((...  67.6 us
    unnamed x3, local copies, waits for them, and re-layouts  2 us

profile of v1, /device:TPU:1, one launch (start us, length us, event | category | flops | bytes accessed | tf_op | source)
XLA Modules:
  0.0 69.6 jit_solution(17568119215918274063)
XLA Ops:
  0.0 0.0 copy-start
  0.0 0.7 copy-done
  0.7 67.6 %multiples.1 = bf16[64,32,512]{2,1,0:T(8,128)(2,1)S(1)} custom-call(bf16[64,32,512]{2,1,0:T(8,128)(2,1)} %rec_in.1, bf16[2304,512]{1,0:T(8,128)(2,1)} %constant.3.tab_in, f32[2,256]{1,0:T(2,128)S(1)} %bitcast.1), custom_call_target="tpu_custom_call" | custom-call | tf_op jit(solution)/shard_map/multiples/pallas_call | solution.py:268
  68.3 1.3 %copy.5 = bf16[64,32,512]{2,1,0:T(8,128)(2,1)} copy(bf16[64,32,512]{2,1,0:T(8,128)(2,1)S(1)} %multiples.1) | data formatting | bytes 4194304
Async XLA Ops:
  0.0 0.7 copy-start

commit v2 on v1

--- a/solution.py
+++ b/solution.py
@@ -29,7 +29,7 @@
     forward = np.stack([cosine, -sine], axis=1).reshape(DEV, 2, 2, NT)
     inverse = np.stack([weight * cosine, -weight * sine], axis=1).reshape(DEV, 2, 2, NT)
     forward = forward.transpose(1, 2, 0, 3).reshape(2 * NF, NT)
-    inverse = inverse.transpose(1, 0, 2, 3).reshape(2 * NF, NT)
+    inverse = inverse.reshape(A, 4, 4, 2, 2, NT).transpose(1, 3, 0, 2, 4, 5).reshape(2 * NF, NT)
     return forward, inverse
 
 
@@ -42,12 +42,12 @@
     return m.reshape(512, 512)
 
 
-def far_first():
-    rnd = np.random.RandomState(7)
-    all_offsets = [(x, y, z, c) for x in range(4) for y in range(4) for z in range(4) for c in range(2)][1:]
-    order = rnd.permutation(len(all_offsets))
-    shuffled = [all_offsets[i] for i in order]
-    return sorted(shuffled, key=lambda o: -sum(min(v, 4 - v) for v in o[:3]))
+def mixed_offsets():
+    offsets = [(x, y, z, c) for x in range(4) for y in range(4) for z in range(4) for c in range(2)][1:]
+    return [offsets[i] for i in np.random.RandomState(1).permutation(len(offsets))]
+
+
+RETURN_ORDER = (2, 0, 1, 3)
 
 
 def nt(left, right):
@@ -59,10 +59,10 @@
 
 
 def kernel(
-    rec_in, tab_in, coef, out,
-    rec, fwd, inv, eye, swap,
-    wide, slab, rbuf, spec, q_a, b_one, b_two, pred, rslab, rret, gath, turned,
-    fs, fr, bs, br, loaded,
+    rec_in, tab_in, coef_in, out,
+    rec, fwd, inv, eye, swap, coef,
+    wide, slab, rbuf, spec, q_a, b_one, b_two, rslab, rret, gath, turned, total,
+    fs, fr, bs, br, loaded, filled,
 ):
     def tab(i):
         return tab_in.at[pl.ds(512 * i, 512)]
@@ -70,10 +70,15 @@
     loads = [
         pltpu.make_async_copy(here, there, loaded.at[i])
         for i, (here, there) in enumerate(
-            [(tab(0), fwd), (rec_in, rec), (tab(2), swap), (tab_in.at[pl.ds(1536, 256), pl.ds(0, 256)], eye), (tab(1), inv)]
+            [(tab(0), fwd), (tab(2), swap), (tab_in.at[pl.ds(1536, 256), pl.ds(0, 256)], eye), (coef_in, coef)]
         )
     ]
-    for load in loads:
+    loads[0].start()
+    for part in range(4):
+        for q in range(4):
+            some = pl.ds(16 * q + 4 * part, 4)
+            pltpu.make_async_copy(rec_in.at[some], rec.at[some], filled.at[part]).start()
+    for load in loads[1:]:
         load.start()
     src, rcv = lax.axis_index("src"), lax.axis_index("rcv")
     me = src * B + rcv
@@ -89,11 +94,11 @@
     y_r = [(v % 2) * 2 for v in ys]
     zs = [lax.rem(z + d, 4) * 2 for d in range(4)]
     cs = [lax.rem(core + d, 2) for d in range(2)]
-    peers = [(zs[o[2]] + y_s[o[1]], xs[o[0]] + y_r[o[1]] + cs[o[3]]) for o in far_first()]
-    for to in peers:
+    offsets = mixed_offsets()
+    peers = [(zs[o[2]] + y_s[o[1]], xs[o[0]] + y_r[o[1]] + cs[o[3]]) for o in offsets]
+    for _, to in sorted(zip(offsets, peers, strict=True), key=lambda p: -sum(min(v, 4 - v) for v in p[0][:3])):
         pl.semaphore_signal(barrier, inc=1, device_id=to, device_id_type=MESH)
     loads[0].wait()
-    loads[1].wait()
 
     def dft(h):
         def step(pair, carry):
@@ -107,7 +112,13 @@
                     ]
             return carry
 
-        lax.fori_loop(0, 8, step, 0, unroll=4)
+        if h == 0:
+            for part in range(4):
+                pltpu.make_async_copy(rec.at[pl.ds(0, 16)], rec.at[pl.ds(0, 16)], filled.at[part]).wait()
+                for pair in range(2):
+                    step(2 * part + pair, 0)
+        else:
+            lax.fori_loop(0, 8, step, 0, unroll=4)
 
         def pack(i, carry):
             for c in range(2):
@@ -135,21 +146,34 @@
     forward_sends(0)
     dft(1)
     forward_sends(1)
-    loads[2].wait()
-    loads[3].wait()
+    for h in range(2):
+        for p, d in enumerate(RETURN_ORDER):
+            at = pl.multiple_of((lax.rem(x + 4 - d, 4) * 2 + h) * 64 + 512, 64)
+            pltpu.make_async_copy(
+                tab_in.at[pl.ds(at, 64)], inv.at[pl.ds(256 * h + 64 * p, 64)], filled.at[4]
+            ).start()
+    for load in loads[1:]:
+        load.wait()
+    pltpu.make_async_copy(inv, inv, filled.at[4]).wait()
 
     norm = 1.0 / math.sqrt(NS)
 
     def middle(h, carry):
         pltpu.make_async_copy(rbuf.at[h], rbuf.at[h], fr.at[h]).wait()
         for c in range(2):
+            piece = jnp.concatenate(
+                [
+                    jnp.concatenate([rbuf[h, :, 4 * bb + k, c].reshape(128, 128) for k in range(4)], axis=1)
+                    for bb in range(4)
+                ],
+                axis=0,
+            )
+            s = nn(piece, swap[...]).astype(BF)
             for bb in range(4):
-                piece = jnp.concatenate(
-                    [rbuf[h, :, 4 * bb + k, c].reshape(128, 128) for k in range(4)], axis=1
-                )
-                s = nn(piece, swap[...]).astype(BF)
                 for q in range(4):
-                    spec[c, :, q, :, 128 * bb : 128 * (bb + 1)] = s[:, 128 * q : 128 * (q + 1)].reshape(A, 16, 128)
+                    spec[c, :, q, :, 128 * bb : 128 * (bb + 1)] = s[
+                        128 * bb : 128 * (bb + 1), 128 * q : 128 * (q + 1)
+                    ].reshape(A, 16, 128)
         for c in range(2):
             for m in range(2):
                 for n in range(2):
@@ -170,7 +194,8 @@
         k_r, k_i = coef[0, at] * norm, coef[1, at] * norm
 
         def scaled(o):
-            r, i = o[:, :512], o[:, 512:]
+            half = o.shape[1] // 2
+            r, i = o[:, :half], o[:, half:]
             return k_r * r - k_i * i, k_r * i + k_i * r
 
         def product(source, target):
@@ -189,65 +214,71 @@
         product(b_one, b_two)
         product(b_two, b_one)
 
-        def last(m, carry2):
-            at_m = pl.multiple_of(m * 256, 256)
-            third = scaled(nn(q_a[pl.ds(at_m, 256), :], b_one[...]))
+        for p, d in enumerate(RETURN_ORDER):
+            bb = lax.rem(x + d, 4)
+            cols = [pl.ds(pl.multiple_of(512 * c + 128 * bb, 128), 128) for c in range(2)]
+            third = scaled(nn(q_a[...], jnp.concatenate([b_one[:, cols[0]], b_one[:, cols[1]]], axis=1)))
+            pieces = []
             for c in range(2):
-                cols = slice(512 * c, 512 * (c + 1))
-                total = b_two[pl.ds(at_m, 256), cols].astype(F32) + b_one[pl.ds(at_m, 256), cols].astype(F32) + third[c]
-                pred[c, pl.ds(m * 4, 4)] = total.astype(BF).reshape(4, 4, 16, 512)
-            return carry2
-
-        lax.fori_loop(0, 2, last, 0)
-
-        for c in range(2):
-            for bb in range(4):
-                piece = jnp.concatenate(
-                    [pred[c, :, q, :, 128 * bb : 128 * (bb + 1)].reshape(128, 128) for q in range(4)], axis=1
-                )
-                s = nn(piece, swap[...]).astype(BF)
+                summed = b_two[0:512, cols[c]].astype(F32) + b_one[0:512, cols[c]].astype(F32) + third[c]
+                summed = summed.astype(BF).reshape(A, 4, 16, 128)
+                pieces.append(jnp.concatenate([summed[:, q].reshape(128, 128) for q in range(4)], axis=1))
+            s = nn(jnp.concatenate(pieces, axis=0), swap[...]).astype(BF)
+            for c in range(2):
                 for k in range(4):
-                    rslab[h, :, 4 * bb + k, c] = s[:, 128 * k : 128 * (k + 1)].reshape(A, 16, 128)
-        mine = pltpu.make_async_copy(rslab.at[h, src, rcv], rret.at[h, me], br.at[h])
-        mine.start()
-        for a, b in peers:
-            pltpu.make_async_remote_copy(
-                src_ref=rslab.at[h, a, b],
-                dst_ref=rret.at[h, me],
-                send_sem=bs.at[h],
-                recv_sem=br.at[h],
-                device_id=(a, b),
-                device_id_type=MESH,
-            ).start()
+                    rslab[h, :, 4 * bb + k, c] = s[128 * c : 128 * (c + 1), 128 * k : 128 * (k + 1)].reshape(A, 16, 128)
+            if p % 2 == 0:
+                continue
+            for e in RETURN_ORDER[p - 1 : p + 1]:
+                there = rret.at[h, RETURN_ORDER.index(e), src * 4 + rcv % 4]
+                if e == 0:
+                    pltpu.make_async_copy(rslab.at[h, src, rcv], there, br.at[h, p // 2]).start()
+            for o, (a, b) in zip(offsets, peers, strict=True):
+                if o[0] in RETURN_ORDER[p - 1 : p + 1]:
+                    pltpu.make_async_remote_copy(
+                        src_ref=rslab.at[h, a, b],
+                        dst_ref=rret.at[h, RETURN_ORDER.index(o[0]), src * 4 + rcv % 4],
+                        send_sem=bs.at[h],
+                        recv_sem=br.at[h, p // 2],
+                        device_id=(a, b),
+                        device_id_type=MESH,
+                    ).start()
         return carry
 
     lax.fori_loop(0, 2, middle, 0)
 
-    def gather(h, carry):
-        pltpu.make_async_copy(rret.at[h], rret.at[h], br.at[h]).wait()
-
-        def widen(i, carry2):
-            gath[pl.ds(pl.multiple_of(i * 512, 512), 512), :] = rret[h, pl.ds(i * 16, 16)].reshape(512, 128).astype(F32)
-            return carry2
-
-        lax.fori_loop(0, 8, widen, 0, unroll=2)
-
-        def turn(j, carry2):
-            w = gath[pl.ds(j, 256, stride=16), :].astype(BF)
-            turned[h, pl.ds(pl.multiple_of(j * 128, 128), 128), :] = nt(eye[0:128, 0:128], w).astype(BF)
-            return carry2
+    def gather(h, pair):
+        pltpu.make_async_copy(
+            rret.at[h, pl.ds(2 * pair, 2)], rret.at[h, pl.ds(2 * pair, 2)], br.at[h, pair]
+        ).wait()
+        for i in range(8):
+            v = rret[h, 2 * pair + i // 4, 8 * (i % 4) : 8 * (i % 4 + 1)]
+            gath[256 * i : 256 * (i + 1), :] = v.reshape(256, 128).astype(F32)
+
+        def turn(j, carry):
+            w = gath[pl.ds(j, 128, stride=16), :].astype(BF)
+            turned[h, pl.ds(pl.multiple_of(j * 128, 128), 128), 128 * pair : 128 * (pair + 1)] = nt(
+                eye[0:128, 0:128], w
+            ).astype(BF)
+            return carry
 
         lax.fori_loop(0, 16, turn, 0, unroll=8)
+
+    gather(0, 0)
+    gather(0, 1)
+
+    def first_half(i, carry):
+        at = pl.ds(pl.multiple_of(i * 256, 256), 256)
+        total[at, :] = nn(turned[0, at, :], inv[0:256, :])
         return carry
 
-    lax.fori_loop(0, 2, gather, 0)
-
-    loads[4].wait()
+    lax.fori_loop(0, 8, first_half, 0, unroll=4)
+    gather(1, 0)
+    gather(1, 1)
 
     def inverse(pair, carry):
-        at = pl.multiple_of(pair * 256, 256)
-        o = nn(turned[0, pl.ds(at, 256), :], inv[0:256, :]) + nn(turned[1, pl.ds(at, 256), :], inv[256:512, :])
-        o = o.astype(BF)
+        at = pl.ds(pl.multiple_of(pair * 256, 256), 256)
+        o = (total[at, :] + nn(turned[1, at, :], inv[256:512, :])).astype(BF)
         for jj in range(2):
             for q in range(4):
                 out[16 * q + 2 * pair + jj] = o[128 * jj + 32 * q : 128 * jj + 32 * (q + 1), :]
@@ -258,7 +289,7 @@
     whole = pl.ds(0, DEV - 1)
     for h in range(2):
         pltpu.make_async_copy(slab.at[h, whole], slab.at[h, whole], fs.at[h]).wait()
-        pltpu.make_async_copy(rret.at[h, whole], rret.at[h, whole], bs.at[h]).wait()
+        pltpu.make_async_copy(slab.at[h, whole], slab.at[h, whole], bs.at[h]).wait()
 
 
 def local(records, surface_operator):
@@ -269,7 +300,7 @@
         kernel,
         name="multiples",
         out_shape=jax.ShapeDtypeStruct((64, 32, NT), BF),
-        in_specs=[pl.BlockSpec(memory_space=pl.ANY)] * 2 + [pl.BlockSpec(memory_space=pltpu.SMEM)],
+        in_specs=[pl.BlockSpec(memory_space=pl.ANY)] * 3,
         out_specs=vmem,
         scratch_shapes=[
             pltpu.VMEM((64, 32, NT), BF),
@@ -277,6 +308,7 @@
             pltpu.VMEM((2 * NF, NT), BF),
             pltpu.VMEM((256, 256), BF),
             pltpu.VMEM((512, 512), BF),
+            pltpu.SMEM((2, NF), F32),
             pltpu.VMEM((2, 2048, 128), F32),
             pltpu.VMEM((2, DEV, 2, 16, 128), BF),
             pltpu.VMEM((2, A, B, 2, 16, 128), BF),
@@ -284,15 +316,16 @@
             pltpu.VMEM((512, 1024), BF),
             pltpu.VMEM((1024, 1024), BF),
             pltpu.VMEM((1024, 1024), BF),
-            pltpu.VMEM((2, A, 4, 16, 512), BF),
             pltpu.VMEM((2, A, B, 2, 16, 128), BF),
-            pltpu.VMEM((2, DEV, 2, 16, 128), BF),
-            pltpu.VMEM((4096, 128), F32),
+            pltpu.VMEM((2, 4, 32, 2, 16, 128), BF),
+            pltpu.VMEM((2048, 128), F32),
             pltpu.VMEM((2, 2048, 256), BF),
+            pltpu.VMEM((2048, NT), F32),
             pltpu.SemaphoreType.DMA((2,)),
             pltpu.SemaphoreType.DMA((2,)),
             pltpu.SemaphoreType.DMA((2,)),
-            pltpu.SemaphoreType.DMA((2,)),
+            pltpu.SemaphoreType.DMA((2, 2)),
+            pltpu.SemaphoreType.DMA((4,)),
             pltpu.SemaphoreType.DMA((5,)),
         ],
         compiler_params=pltpu.CompilerParams(

time: 69.7 us -> 63.8 us (0.915)
  Pallas kernels: 67.6 us -> 61.6 us
    pallas_call x1, Pallas kernels: 67.6 us -> 61.6 us  [local(): pl.pallas_call(kernel, name='multiples', out_shape=jax.ShapeDtypeStruct((...]
where the time goes in v2:
time: 63.8 us; the launch traced here: 63.6 us
  Pallas kernels  61.6 us (97%)
  local copies, waits for them, and re-layouts  2 us (3%)
    pallas_call x1, Pallas kernels, local(): pl.pallas_call(kernel, name='multiples', out_shape=jax.ShapeDtypeStruct((...  61.6 us
    unnamed x3, local copies, waits for them, and re-layouts  2 us

profile of v2, /device:TPU:1, one launch (start us, length us, event | category | flops | bytes accessed | tf_op | source)
XLA Modules:
  0.0 63.6 jit_solution(4303533716561686090)
XLA Ops:
  0.0 0.0 copy-start
  0.0 0.7 %copy-done = f32[256,2]{0,1:T(2,128)S(1)} copy-done((f32[256,2]{0,1:T(2,128)S(1)}, f32[256,2]{0,1:T(2,128)}, u32[]{:S(2)}) %copy-start) | copy-done | bytes 2072
  0.7 61.6 %multiples.1 = bf16[64,32,512]{2,1,0:T(8,128)(2,1)S(1)} custom-call(bf16[64,32,512]{2,1,0:T(8,128)(2,1)} %rec_in.1, bf16[2304,512]{1,0:T(8,128)(2,1)} %constant.3.tab_in, f32[2,256]{1,0:T(2,128)S(1)} %bitcast.1), custom_call_target="tpu_custom_call" | custom-call | tf_op jit(solution)/shard_map/multiples/pallas_call | solution.py:299
  62.2 1.3 %copy.5 = bf16[64,32,512]{2,1,0:T(8,128)(2,1)} copy(bf16[64,32,512]{2,1,0:T(8,128)(2,1)S(1)} %multiples.1) | data formatting | bytes 4194304
Async XLA Ops:
  0.0 0.7 %copy-start = (f32[256,2]{0,1:T(2,128)S(1)}, f32[256,2]{0,1:T(2,128)}, u32[]{:S(2)}) copy-start(f32[256,2]{0,1:T(2,128)} %param.4) | copy-start | bytes 6148

commit v3 on v2

--- a/solution.py
+++ b/solution.py
@@ -59,9 +59,9 @@
 
 
 def kernel(
-    rec_in, tab_in, coef_in, out,
-    rec, fwd, inv, eye, swap, coef,
-    wide, slab, rbuf, spec, q_a, b_one, b_two, rslab, rret, gath, turned, total,
+    rec_in, tab_in, coef_in, total, late, inv_late,
+    rec, fwd, inv_early, eye, swap, coef,
+    wide, slab, rbuf, spec, q_a, b_one, b_two, rslab, rret, gath, early,
     fs, fr, bs, br, loaded, filled,
 ):
     def tab(i):
@@ -115,10 +115,7 @@
         if h == 0:
             for part in range(4):
                 pltpu.make_async_copy(rec.at[pl.ds(0, 16)], rec.at[pl.ds(0, 16)], filled.at[part]).wait()
-                for pair in range(2):
-                    step(2 * part + pair, 0)
-        else:
-            lax.fori_loop(0, 8, step, 0, unroll=4)
+        lax.fori_loop(0, 8, step, 0, unroll=8)
 
         def pack(i, carry):
             for c in range(2):
@@ -131,7 +128,7 @@
     def forward_sends(h):
         mine = pltpu.make_async_copy(slab.at[h, me], rbuf.at[h, src, rcv], fr.at[h])
         mine.start()
-        for a, b in peers:
+        for _, (a, b) in sorted(zip(offsets, peers, strict=True), key=lambda p: -sum(min(v, 4 - v) for v in p[0][:3])) if h == 0 else zip(offsets, peers, strict=True):
             pltpu.make_async_remote_copy(
                 src_ref=slab.at[h, a * B + b],
                 dst_ref=rbuf.at[h, src, rcv],
@@ -150,11 +147,12 @@
         for p, d in enumerate(RETURN_ORDER):
             at = pl.multiple_of((lax.rem(x + 4 - d, 4) * 2 + h) * 64 + 512, 64)
             pltpu.make_async_copy(
-                tab_in.at[pl.ds(at, 64)], inv.at[pl.ds(256 * h + 64 * p, 64)], filled.at[4]
+                tab_in.at[pl.ds(at, 64)], (inv_late if h else inv_early).at[pl.ds(64 * p, 64)], filled.at[4 + h]
             ).start()
     for load in loads[1:]:
         load.wait()
-    pltpu.make_async_copy(inv, inv, filled.at[4]).wait()
+    pltpu.make_async_copy(inv_early, inv_early, filled.at[4]).wait()
+    pltpu.make_async_copy(inv_late, inv_late, filled.at[5]).wait()
 
     norm = 1.0 / math.sqrt(NS)
 
@@ -233,7 +231,7 @@
                 there = rret.at[h, RETURN_ORDER.index(e), src * 4 + rcv % 4]
                 if e == 0:
                     pltpu.make_async_copy(rslab.at[h, src, rcv], there, br.at[h, p // 2]).start()
-            for o, (a, b) in zip(offsets, peers, strict=True):
+            for o, (a, b) in sorted(zip(offsets, peers, strict=True), key=lambda p: -sum(min(v, 4 - v) for v in p[0][:3])):
                 if o[0] in RETURN_ORDER[p - 1 : p + 1]:
                     pltpu.make_async_remote_copy(
                         src_ref=rslab.at[h, a, b],
@@ -247,7 +245,7 @@
 
     lax.fori_loop(0, 2, middle, 0)
 
-    def gather(h, pair):
+    def gather(h, pair, turned):
         pltpu.make_async_copy(
             rret.at[h, pl.ds(2 * pair, 2)], rret.at[h, pl.ds(2 * pair, 2)], br.at[h, pair]
         ).wait()
@@ -257,34 +255,24 @@
 
         def turn(j, carry):
             w = gath[pl.ds(j, 128, stride=16), :].astype(BF)
-            turned[h, pl.ds(pl.multiple_of(j * 128, 128), 128), 128 * pair : 128 * (pair + 1)] = nt(
+            turned[pl.ds(pl.multiple_of(j * 128, 128), 128), 128 * pair : 128 * (pair + 1)] = nt(
                 eye[0:128, 0:128], w
             ).astype(BF)
             return carry
 
         lax.fori_loop(0, 16, turn, 0, unroll=8)
 
-    gather(0, 0)
-    gather(0, 1)
+    gather(0, 0, early)
+    gather(0, 1, early)
 
     def first_half(i, carry):
         at = pl.ds(pl.multiple_of(i * 256, 256), 256)
-        total[at, :] = nn(turned[0, at, :], inv[0:256, :])
+        total[at, :] = nn(early[at, :], inv_early[...])
         return carry
 
     lax.fori_loop(0, 8, first_half, 0, unroll=4)
-    gather(1, 0)
-    gather(1, 1)
-
-    def inverse(pair, carry):
-        at = pl.ds(pl.multiple_of(pair * 256, 256), 256)
-        o = (total[at, :] + nn(turned[1, at, :], inv[256:512, :])).astype(BF)
-        for jj in range(2):
-            for q in range(4):
-                out[16 * q + 2 * pair + jj] = o[128 * jj + 32 * q : 128 * jj + 32 * (q + 1), :]
-        return carry
-
-    lax.fori_loop(0, 8, inverse, 0, unroll=4)
+    gather(1, 0, late)
+    gather(1, 1, late)
 
     whole = pl.ds(0, DEV - 1)
     for h in range(2):
@@ -292,20 +280,38 @@
         pltpu.make_async_copy(slab.at[h, whole], slab.at[h, whole], bs.at[h]).wait()
 
 
+def finish(total, late, inv_late, out, done, sem):
+    copies = []
+    for i in range(8):
+        at = slice(256 * i, 256 * (i + 1))
+        o = (total[at, :] + nn(late[at, :], inv_late[...])).astype(BF).reshape(2, 4, 32, NT)
+        for jj in range(2):
+            done[:, 2 * i + jj] = o[jj]
+        copies.append(pltpu.make_async_copy(done.at[:, pl.ds(2 * i, 2)], out.at[:, pl.ds(2 * i, 2)], sem.at[i]))
+        copies[-1].start()
+    for copy in copies:
+        copy.wait()
+
+
 def local(records, surface_operator):
     forward, inverse = tables()
-    packed = np.concatenate([forward, inverse, swap_matrix(), np.eye(768, 512, dtype=np.float32)])
+    packed = np.concatenate([forward, inverse, swap_matrix(), np.eye(256, 512, dtype=np.float32)])
+    packed = jnp.asarray(packed).astype(BF)
     vmem = pl.BlockSpec(memory_space=pltpu.VMEM)
-    return pl.pallas_call(
+    total, late, inv_late = pl.pallas_call(
         kernel,
         name="multiples",
-        out_shape=jax.ShapeDtypeStruct((64, 32, NT), BF),
+        out_shape=[
+            jax.ShapeDtypeStruct((2048, NT), F32),
+            jax.ShapeDtypeStruct((2048, NF), BF),
+            jax.ShapeDtypeStruct((NF, NT), BF),
+        ],
         in_specs=[pl.BlockSpec(memory_space=pl.ANY)] * 3,
-        out_specs=vmem,
+        out_specs=[vmem] * 3,
         scratch_shapes=[
             pltpu.VMEM((64, 32, NT), BF),
             pltpu.VMEM((2 * NF, NT), BF),
-            pltpu.VMEM((2 * NF, NT), BF),
+            pltpu.VMEM((NF, NT), BF),
             pltpu.VMEM((256, 256), BF),
             pltpu.VMEM((512, 512), BF),
             pltpu.SMEM((2, NF), F32),
@@ -319,19 +325,28 @@
             pltpu.VMEM((2, A, B, 2, 16, 128), BF),
             pltpu.VMEM((2, 4, 32, 2, 16, 128), BF),
             pltpu.VMEM((2048, 128), F32),
-            pltpu.VMEM((2, 2048, 256), BF),
-            pltpu.VMEM((2048, NT), F32),
+            pltpu.VMEM((2048, NF), BF),
             pltpu.SemaphoreType.DMA((2,)),
             pltpu.SemaphoreType.DMA((2,)),
             pltpu.SemaphoreType.DMA((2,)),
             pltpu.SemaphoreType.DMA((2, 2)),
             pltpu.SemaphoreType.DMA((4,)),
-            pltpu.SemaphoreType.DMA((5,)),
+            pltpu.SemaphoreType.DMA((6,)),
         ],
         compiler_params=pltpu.CompilerParams(
-            collective_id=0, has_side_effects=True, vmem_limit_bytes=50 * 1024 * 1024 + 512 * 1024
+            collective_id=0, has_side_effects=True, vmem_limit_bytes=40 * 1024 * 1024
         ),
-    )(records, jnp.asarray(packed).astype(BF), surface_operator.T)
+    )(*[pltpu.with_memory_space_constraint(v, pltpu.HBM) for v in (records, packed, surface_operator.T)])
+    multiples = pl.pallas_call(
+        finish,
+        name="finish",
+        out_shape=jax.ShapeDtypeStruct((4, 16, 32, NT), BF),
+        in_specs=[vmem] * 3,
+        out_specs=pl.BlockSpec(memory_space=pl.ANY),
+        scratch_shapes=[pltpu.VMEM((4, 16, 32, NT), BF), pltpu.SemaphoreType.DMA((8,))],
+        compiler_params=pltpu.CompilerParams(vmem_limit_bytes=16 * 1024 * 1024),
+    )(total, late, inv_late)
+    return multiples.reshape(64, 32, NT)
 
 
 def solution(mesh):

time: 63.8 us -> 62.1 us (0.973)
  local copies, waits for them, and re-layouts: 2 us -> 0 us
    unnamed x3 -> x0, local copies, waits for them, and re-layouts: 2 us -> none
    pallas_call x1 -> x2, Pallas kernels: 61.6 us -> 61.9 us  [the longest x1 60.3 us: local(): pl.pallas_call(kernel, name='multiples', out_shape=[jax.ShapeDtypeStruct(...]
where the time goes in v3:
time: 62.1 us; the launch traced here: 61.9 us
  Pallas kernels  61.9 us (100%)
    pallas_call x1, Pallas kernels, local(): pl.pallas_call(kernel, name='multiples', out_shape=[jax.ShapeDtypeStruct(...  60.3 us
    pallas_call x1, Pallas kernels, local(): pl.pallas_call(finish, name='finish', out_shape=jax.ShapeDtypeStruct((4,...  1.61 us

profile of v3, /device:TPU:1, one launch (start us, length us, event | category | flops | bytes accessed | tf_op | source)
XLA Modules:
  0.0 61.9 jit_solution(5339672043516342632)
XLA Ops:
  0.0 60.3 %multiples.1 = (f32[2048,512]{1,0:T(8,128)S(1)}, bf16[2048,256]{1,0:T(8,128)(2,1)S(1)}, bf16[256,512]{1,0:T(8,128)(2,1)S(1)}) custom-call(bf16[64,32,512]{2,1,0:T(8,128)(2,1)} %rec_in.1, bf16[1792,512]{1,0:T(8,128)(2,1)} %constant.3.tab_in, f32[2,256]{1,0:T(2,128)} %bitcast.2), custom_call_target="tpu_custom_call" | custom-call | tf_op jit(solution)/shard_map/multiples/pallas_call | solution.py:301
  60.3 1.6 %finish.1 = bf16[4,16,32,512]{3,2,1,0:T(8,128)(2,1)} custom-call(f32[2048,512]{1,0:T(8,128)S(1)} %get-tuple-element.8.total, bf16[2048,256]{1,0:T(8,128)(2,1)S(1)} %get-tuple-element.9.late, bf16[256,512]{1,0:T(8,128)(2,1)S(1)} %get-tuple-element.10.inv_late), custom_call_target="tpu_custom_call" | custom-call | tf_op jit(solution)/shard_map/finish/pallas_call | solution.py:340

commit v4 on v3

--- a/solution.py
+++ b/solution.py
@@ -47,7 +47,7 @@
     return [offsets[i] for i in np.random.RandomState(1).permutation(len(offsets))]
 
 
-RETURN_ORDER = (2, 0, 1, 3)
+RETURN_ORDER = (2, 1, 0, 3)
 
 
 def nt(left, right):

time: 62.1 us -> 61.6 us (level)
  no operation moved by 1% of the time
where the time goes in v4:
time: 61.6 us; the launch traced here: 61.5 us
  Pallas kernels  61.4 us (100%)
    pallas_call x1, Pallas kernels, local(): pl.pallas_call(kernel, name='multiples', out_shape=[jax.ShapeDtypeStruct(...  59.8 us
    pallas_call x1, Pallas kernels, local(): pl.pallas_call(finish, name='finish', out_shape=jax.ShapeDtypeStruct((4,...  1.61 us

profile of v4, /device:TPU:1, one launch (start us, length us, event | category | flops | bytes accessed | tf_op | source)
XLA Modules:
  0.0 61.5 jit_solution(7622330211722212344)
XLA Ops:
  0.0 59.8 %multiples.1 = (f32[2048,512]{1,0:T(8,128)S(1)}, bf16[2048,256]{1,0:T(8,128)(2,1)S(1)}, bf16[256,512]{1,0:T(8,128)(2,1)S(1)}) custom-call(bf16[64,32,512]{2,1,0:T(8,128)(2,1)} %rec_in.1, bf16[1792,512]{1,0:T(8,128)(2,1)} %constant.3.tab_in, f32[2,256]{1,0:T(2,128)} %bitcast.2), custom_call_target="tpu_custom_call" | custom-call | tf_op jit(solution)/shard_map/multiples/pallas_call | solution.py:301
  59.8 1.6 %finish.1 = bf16[4,16,32,512]{3,2,1,0:T(8,128)(2,1)} custom-call(f32[2048,512]{1,0:T(8,128)S(1)} %get-tuple-element.8.total, bf16[2048,256]{1,0:T(8,128)(2,1)S(1)} %get-tuple-element.9.late, bf16[256,512]{1,0:T(8,128)(2,1)S(1)} %get-tuple-element.10.inv_late), custom_call_target="tpu_custom_call" | custom-call | tf_op jit(solution)/shard_map/finish/pallas_call | solution.py:340

commit v5 on v4

--- a/solution.py
+++ b/solution.py
@@ -74,12 +74,8 @@
         )
     ]
     loads[0].start()
-    for part in range(4):
-        for q in range(4):
-            some = pl.ds(16 * q + 4 * part, 4)
-            pltpu.make_async_copy(rec_in.at[some], rec.at[some], filled.at[part]).start()
-    for load in loads[1:]:
-        load.start()
+    traces_in = pltpu.make_async_copy(rec_in, rec, filled.at[0])
+    traces_in.start()
     src, rcv = lax.axis_index("src"), lax.axis_index("rcv")
     me = src * B + rcv
     z, y_hi = src // 2, src % 2
@@ -98,7 +94,10 @@
     peers = [(zs[o[2]] + y_s[o[1]], xs[o[0]] + y_r[o[1]] + cs[o[3]]) for o in offsets]
     for _, to in sorted(zip(offsets, peers, strict=True), key=lambda p: -sum(min(v, 4 - v) for v in p[0][:3])):
         pl.semaphore_signal(barrier, inc=1, device_id=to, device_id_type=MESH)
+    for load in loads[1:]:
+        load.start()
     loads[0].wait()
+    traces_in.wait()
 
     def dft(h):
         def step(pair, carry):
@@ -112,9 +111,6 @@
                     ]
             return carry
 
-        if h == 0:
-            for part in range(4):
-                pltpu.make_async_copy(rec.at[pl.ds(0, 16)], rec.at[pl.ds(0, 16)], filled.at[part]).wait()
         lax.fori_loop(0, 8, step, 0, unroll=8)
 
         def pack(i, carry):
@@ -123,7 +119,7 @@
                 slab[h, pl.ds(i * 16, 16), c] = v.astype(BF).reshape(16, 16, 128)
             return carry
 
-        lax.fori_loop(0, 8, pack, 0, unroll=2)
+        lax.fori_loop(0, 8, pack, 0, unroll=4)
 
     def forward_sends(h):
         mine = pltpu.make_async_copy(slab.at[h, me], rbuf.at[h, src, rcv], fr.at[h])
@@ -147,12 +143,12 @@
         for p, d in enumerate(RETURN_ORDER):
             at = pl.multiple_of((lax.rem(x + 4 - d, 4) * 2 + h) * 64 + 512, 64)
             pltpu.make_async_copy(
-                tab_in.at[pl.ds(at, 64)], (inv_late if h else inv_early).at[pl.ds(64 * p, 64)], filled.at[4 + h]
+                tab_in.at[pl.ds(at, 64)], (inv_late if h else inv_early).at[pl.ds(64 * p, 64)], filled.at[1 + h]
             ).start()
     for load in loads[1:]:
         load.wait()
-    pltpu.make_async_copy(inv_early, inv_early, filled.at[4]).wait()
-    pltpu.make_async_copy(inv_late, inv_late, filled.at[5]).wait()
+    pltpu.make_async_copy(inv_early, inv_early, filled.at[1]).wait()
+    pltpu.make_async_copy(inv_late, inv_late, filled.at[2]).wait()
 
     norm = 1.0 / math.sqrt(NS)
 
@@ -260,7 +256,7 @@
             ).astype(BF)
             return carry
 
-        lax.fori_loop(0, 16, turn, 0, unroll=8)
+        lax.fori_loop(0, 16, turn, 0, unroll=16)
 
     gather(0, 0, early)
     gather(0, 1, early)
@@ -331,7 +327,7 @@
             pltpu.SemaphoreType.DMA((2,)),
             pltpu.SemaphoreType.DMA((2, 2)),
             pltpu.SemaphoreType.DMA((4,)),
-            pltpu.SemaphoreType.DMA((6,)),
+            pltpu.SemaphoreType.DMA((3,)),
         ],
         compiler_params=pltpu.CompilerParams(
             collective_id=0, has_side_effects=True, vmem_limit_bytes=40 * 1024 * 1024

time: 61.6 us -> 61.3 us (level)
  no operation moved by 1% of the time
where the time goes in v5:
time: 61.3 us; the launch traced here: 61.1 us
  Pallas kernels  61.1 us (100%)
    pallas_call x1, Pallas kernels, local(): pl.pallas_call(kernel, name='multiples', out_shape=[jax.ShapeDtypeStruct(...  59.5 us
    pallas_call x1, Pallas kernels, local(): pl.pallas_call(finish, name='finish', out_shape=jax.ShapeDtypeStruct((4,...  1.61 us

profile of v5, /device:TPU:1, one launch (start us, length us, event | category | flops | bytes accessed | tf_op | source)
XLA Modules:
  0.0 61.1 jit_solution(10899655390510264902)
XLA Ops:
  0.0 59.5 %multiples.1 = (f32[2048,512]{1,0:T(8,128)S(1)}, bf16[2048,256]{1,0:T(8,128)(2,1)S(1)}, bf16[256,512]{1,0:T(8,128)(2,1)S(1)}) custom-call(bf16[64,32,512]{2,1,0:T(8,128)(2,1)} %rec_in.1, bf16[1792,512]{1,0:T(8,128)(2,1)} %constant.3.tab_in, f32[2,256]{1,0:T(2,128)} %bitcast.2), custom_call_target="tpu_custom_call" | custom-call | tf_op jit(solution)/shard_map/multiples/pallas_call | solution.py:297
  59.5 1.6 %finish.1 = bf16[4,16,32,512]{3,2,1,0:T(8,128)(2,1)} custom-call(f32[2048,512]{1,0:T(8,128)S(1)} %get-tuple-element.8.total, bf16[2048,256]{1,0:T(8,128)(2,1)S(1)} %get-tuple-element.9.late, bf16[256,512]{1,0:T(8,128)(2,1)S(1)} %get-tuple-element.10.inv_late), custom_call_target="tpu_custom_call" | custom-call | tf_op jit(solution)/shard_map/finish/pallas_call | solution.py:336

commit v6 on v5

--- a/solution.py
+++ b/solution.py
@@ -266,7 +266,7 @@
         total[at, :] = nn(early[at, :], inv_early[...])
         return carry
 
-    lax.fori_loop(0, 8, first_half, 0, unroll=4)
+    lax.fori_loop(0, 8, first_half, 0, unroll=8)
     gather(1, 0, late)
     gather(1, 1, late)
 
@@ -278,12 +278,10 @@
 
 def finish(total, late, inv_late, out, done, sem):
     copies = []
-    for i in range(8):
-        at = slice(256 * i, 256 * (i + 1))
-        o = (total[at, :] + nn(late[at, :], inv_late[...])).astype(BF).reshape(2, 4, 32, NT)
-        for jj in range(2):
-            done[:, 2 * i + jj] = o[jj]
-        copies.append(pltpu.make_async_copy(done.at[:, pl.ds(2 * i, 2)], out.at[:, pl.ds(2 * i, 2)], sem.at[i]))
+    for i in range(16):
+        at = slice(128 * i, 128 * (i + 1))
+        done[:, i] = (total[at, :] + nn(late[at, :], inv_late[...])).astype(BF).reshape(4, 32, NT)
+        copies.append(pltpu.make_async_copy(done.at[:, i], out.at[:, i], sem.at[i]))
         copies[-1].start()
     for copy in copies:
         copy.wait()
@@ -339,7 +337,7 @@
         out_shape=jax.ShapeDtypeStruct((4, 16, 32, NT), BF),
         in_specs=[vmem] * 3,
         out_specs=pl.BlockSpec(memory_space=pl.ANY),
-        scratch_shapes=[pltpu.VMEM((4, 16, 32, NT), BF), pltpu.SemaphoreType.DMA((8,))],
+        scratch_shapes=[pltpu.VMEM((4, 16, 32, NT), BF), pltpu.SemaphoreType.DMA((16,))],
         compiler_params=pltpu.CompilerParams(vmem_limit_bytes=16 * 1024 * 1024),
     )(total, late, inv_late)
     return multiples.reshape(64, 32, NT)

time: 61.3 us -> 61.3 us (level)
  no operation moved by 1% of the time
where the time goes in v6:
time: 61.3 us; the launch traced here: 61.1 us
  Pallas kernels  61.1 us (100%)
    pallas_call x1, Pallas kernels, local(): pl.pallas_call(kernel, name='multiples', out_shape=[jax.ShapeDtypeStruct(...  59.5 us
    pallas_call x1, Pallas kernels, local(): pl.pallas_call(finish, name='finish', out_shape=jax.ShapeDtypeStruct((4,...  1.65 us

profile of v6, /device:TPU:1, one launch (start us, length us, event | category | flops | bytes accessed | tf_op | source)
XLA Modules:
  0.0 61.1 jit_solution(10536121472020780988)
XLA Ops:
  0.0 59.5 %multiples.1 = (f32[2048,512]{1,0:T(8,128)S(1)}, bf16[2048,256]{1,0:T(8,128)(2,1)S(1)}, bf16[256,512]{1,0:T(8,128)(2,1)S(1)}) custom-call(bf16[64,32,512]{2,1,0:T(8,128)(2,1)} %rec_in.1, bf16[1792,512]{1,0:T(8,128)(2,1)} %constant.3.tab_in, f32[2,256]{1,0:T(2,128)} %bitcast.2), custom_call_target="tpu_custom_call" | custom-call | tf_op jit(solution)/shard_map/multiples/pallas_call | solution.py:295
  59.5 1.7 %finish.1 = bf16[4,16,32,512]{3,2,1,0:T(8,128)(2,1)} custom-call(f32[2048,512]{1,0:T(8,128)S(1)} %get-tuple-element.8.total, bf16[2048,256]{1,0:T(8,128)(2,1)S(1)} %get-tuple-element.9.late, bf16[256,512]{1,0:T(8,128)(2,1)S(1)} %get-tuple-element.10.inv_late), custom_call_target="tpu_custom_call" | custom-call | tf_op jit(solution)/shard_map/finish/pallas_call | solution.py:334
